TPU v7x, 128 devices: a whole 4x4x4 slice. The times are simulated.
128 devices in a mesh: ctx: 8 (over z_hi, x), tp: 8 (over y, core), dp: 2 (over z_lo).
Axes of the slice: x: 4, y: 4, z: 4 (z_hi: 2, z_lo: 2; z = z_hi * 2 + z_lo), core: 2. Of those that a mesh axis runs over, the one named last changes fastest.
Arguments:
- queries: bfloat16 [2, 4096, 8192], P('dp', 'ctx', 'tp'), may hold values from -80 to 80, as said below
- keys: bfloat16 [2, 4096, 8192], P('dp', 'ctx', 'tp'), may hold values from -4 to 4
- values: bfloat16 [2, 4096, 8192], P('dp', 'ctx', 'tp'), may hold values from -6 to 6
- bias_u: float32 [8192], P('tp'), may hold values from -3 to 3
- bias_w: float32 [8192], P('tp'), may hold values from -3 to 3
- rel_table: bfloat16 [1024, 8192], P(None, 'tp'), may hold values from -1.1953125 to 1.1953125
- out_weight: bfloat16 [8192, 8192], P('tp', ('ctx', 'dp')), may hold values from -0.0625 to 0.0625
- grad_out: bfloat16 [2, 4096, 8192], P('dp', 'ctx', 'tp'), may hold values from -6 to 6
- doc_lengths: int32 [2, 16], P('dp'), may hold values from 1 to 1024, 4096 in all within a row
Outputs:
- grad_queries: bfloat16 [2, 4096, 8192], P('dp', 'ctx', 'tp')
- grad_keys: bfloat16 [2, 4096, 8192], P('dp', 'ctx', 'tp')
- grad_values: bfloat16 [2, 4096, 8192], P('dp', 'ctx', 'tp')
- grad_table: float32 [1024, 8192], P(None, 'tp')
- grad_biases: float32 [2, 8192], P(None, 'tp')
Inputs may be any that keep to these rules, and one draw needn't show every extreme that they name: Entries of keys lie within the range; row t of a head's queries may be a multiple, up to 20, of its key row t. `doc_lengths`: each row's 16 lengths sum to 4096, and the longest document in each row has 1024 tokens.
All inputs are finite; a program needn't handle non-finite values.
Results may differ from a plain program's by a relative error of at most 0.0074.
Values may be sent and summed in bfloat16 or wider, within the bound.
No kernel may reach another device: no remote copies, remote signals or barrier semaphores. Data moves between devices by JAX's collectives and lax.ppermute only.
A program may use at most 192 MiB of HBM per device.

v0:
```python
import math

import jax
import jax.numpy as jnp
from jax import lax
from jax.sharding import Mesh
from jax.sharding import PartitionSpec as P

HD = 128
CTX_DP = ("ctx_0", "ctx_1", "dp")
CTX = ("ctx_0", "ctx_1")


def laid_out(blocks, dim):
    shape = list(blocks.shape[1:])
    shape[dim] *= blocks.shape[0]
    return jnp.moveaxis(blocks, 0, dim).reshape(shape)


def stacked_from(value, axes, sequence):
    blocks = value
    for k in sequence:
        blocks = lax.all_gather(blocks, axes[k])
    done = sequence[::-1]
    back = [done.index(k) for k in range(len(axes))]
    blocks = blocks.transpose(*back, *range(len(axes), blocks.ndim))
    return blocks.reshape(-1, *value.shape)


def gather_axes(value, axes, sequence, dim):
    return laid_out(stacked_from(value, axes, sequence), dim)


def from_behind(value, axis, steps):
    count = lax.axis_size(axis)
    first, last = (max(0, -steps), min(count, count - steps))
    return lax.ppermute(value, axis, [(source, source + steps) for source in range(first, last)])


def skew_rows(scores_raw, seg_len):
    padded = jnp.pad(scores_raw, ((0, 0), (0, seg_len)))
    flattened = padded.reshape(-1)
    window = lax.slice_in_dim(flattened, seg_len - 1, seg_len - 1 + seg_len * (3 * seg_len - 1))
    return window.reshape(seg_len, 3 * seg_len - 1)[:, : 2 * seg_len]


def unskew_rows(grad_logits, seg_len):
    padded = jnp.pad(grad_logits, ((0, 0), (seg_len - 1, seg_len + 1)))
    flattened = jnp.pad(padded.reshape(-1), (0, seg_len))
    return flattened.reshape(seg_len, 4 * seg_len + 1)[:, : 2 * seg_len]


def head_backward(
    query_rows, keys_all, values_all, grad_rows, bias_u_row, bias_w_row, rel_back, visible
):
    seg_len = query_rows.shape[0]
    score_scale = 1.0 / math.sqrt(query_rows.shape[1])
    query_content = (query_rows.astype(jnp.float32) + bias_u_row).astype(jnp.bfloat16)
    query_position = (query_rows.astype(jnp.float32) + bias_w_row).astype(jnp.bfloat16)
    content = jnp.einsum("id,jd->ij", query_content, keys_all, preferred_element_type=jnp.float32)
    rel_raw = jnp.einsum("id,ed->ie", query_position, rel_back, preferred_element_type=jnp.float32)
    logits = jnp.where(visible, (content + skew_rows(rel_raw, seg_len)) * score_scale, -jnp.inf)
    row_peak = jnp.max(logits, axis=1, keepdims=True)
    raised = jnp.exp(logits - row_peak)
    weights = raised / jnp.sum(raised, axis=1, keepdims=True)
    grad_weights = jnp.einsum(
        "id,jd->ij", grad_rows, values_all, preferred_element_type=jnp.float32
    )
    row_inner = jnp.sum(weights * grad_weights, axis=1, keepdims=True)
    grad_logits = (weights * (grad_weights - row_inner) * score_scale).astype(jnp.bfloat16)
    weights_low = weights.astype(jnp.bfloat16)
    grad_shifted = unskew_rows(grad_logits, seg_len)
    query_content_part = jnp.dot(grad_logits, keys_all, preferred_element_type=jnp.float32)
    query_rel_part = jnp.dot(grad_shifted, rel_back, preferred_element_type=jnp.float32)
    grad_query = (query_content_part + query_rel_part).astype(jnp.bfloat16)
    grad_keys_all = jnp.einsum(
        "ij,id->jd", grad_logits, query_content, preferred_element_type=jnp.float32
    )
    grad_values_all = jnp.einsum(
        "ij,id->jd", weights_low, grad_rows, preferred_element_type=jnp.float32
    )
    grad_rel = jnp.einsum(
        "ie,id->ed", grad_shifted, query_position, preferred_element_type=jnp.float32
    )[::-1]
    return (
        grad_query,
        grad_keys_all,
        grad_values_all,
        grad_rel,
        jnp.sum(query_content_part, axis=0),
        jnp.sum(query_rel_part, axis=0),
    )


def to_heads(rows, head_dim):
    return rows.reshape(rows.shape[0], rows.shape[1] // head_dim, head_dim).transpose(1, 0, 2)


def from_heads(stacked):
    return stacked.transpose(1, 0, 2).reshape(stacked.shape[1], stacked.shape[0] * stacked.shape[2])


def doc_number(positions, doc_ends):
    return jnp.sum((doc_ends[None, :] <= positions[:, None]).astype(jnp.int32), axis=1)


def per_device(queries, keys, values, bias_u, bias_w, rel_table, out_weight, grad_out, doc_lengths):
    seg_len = queries.shape[1]
    head_dim = HD
    cotangent = lax.all_gather(grad_out[0], "tp", axis=1, tiled=True)
    full_weight = gather_axes(out_weight, CTX_DP, (0, 2, 1), 1)
    grad_heads = jnp.einsum("sd,hd->sh", cotangent, full_weight, preferred_element_type=jnp.float32)
    grad_heads = grad_heads.astype(jnp.bfloat16)
    doc_ends = jnp.cumsum(doc_lengths[0])
    seg_start = lax.axis_index(CTX) * seg_len
    query_pos = seg_start + jnp.arange(seg_len, dtype=jnp.int32)
    key_pos = seg_start - seg_len + jnp.arange(2 * seg_len, dtype=jnp.int32)
    row_ids = jnp.arange(seg_len, dtype=jnp.int32)[:, None]
    col_ids = jnp.arange(2 * seg_len, dtype=jnp.int32)[None, :]
    visible = (
        (key_pos[None, :] >= 0)
        & (col_ids <= row_ids + seg_len)
        & (doc_number(key_pos, doc_ends)[None, :] == doc_number(query_pos, doc_ends)[:, None])
    )
    stacked = (
        to_heads(queries[0], head_dim),
        to_heads(keys[0], head_dim),
        to_heads(values[0], head_dim),
        to_heads(grad_heads, head_dim),
        bias_u.reshape(-1, head_dim),
        bias_w.reshape(-1, head_dim),
        to_heads(rel_table[::-1], head_dim),
    )
    memory_keys, memory_values = from_behind((keys[0], values[0]), CTX, 1)
    stacked = stacked + (to_heads(memory_keys, head_dim), to_heads(memory_values, head_dim))

    def per_head(packed):
        query_rows, key_rows, value_rows, grad_rows, bias_u_row, bias_w_row, rel_rows = packed[:7]
        head_memory_keys, head_memory_values = (packed[7], packed[8])
        keys_all = jnp.concatenate([head_memory_keys, key_rows], axis=0)
        values_all = jnp.concatenate([head_memory_values, value_rows], axis=0)
        grad_query, grad_keys_all, grad_values_all, grad_rel, grad_u, grad_w = head_backward(
            query_rows, keys_all, values_all, grad_rows, bias_u_row, bias_w_row, rel_rows, visible
        )
        own_keys = grad_keys_all[seg_len:]
        own_values = grad_values_all[seg_len:]
        return (
            grad_query,
            own_keys,
            own_values,
            grad_keys_all[:seg_len],
            grad_values_all[:seg_len],
            grad_rel,
            grad_u,
            grad_w,
        )

    (
        grad_query_heads,
        own_keys,
        own_values,
        memory_key_grads,
        memory_value_grads,
        grad_rel,
        grad_u,
        grad_w,
    ) = lax.map(per_head, stacked)
    back_keys, back_values = from_behind((memory_key_grads, memory_value_grads), CTX, -1)
    own_keys = own_keys + back_keys
    own_values = own_values + back_values
    bias_terms = jnp.stack([grad_u.reshape(-1), grad_w.reshape(-1)])
    grad_table, grad_biases = lax.psum((from_heads(grad_rel), bias_terms), CTX_DP)
    grad_queries = from_heads(grad_query_heads)[None]
    grad_keys = from_heads(own_keys).astype(jnp.bfloat16)[None]
    grad_values = from_heads(own_values).astype(jnp.bfloat16)[None]
    return (grad_queries, grad_keys, grad_values, grad_table, grad_biases)


def solution(mesh):
    torus = Mesh(
        mesh.devices.reshape(2, 4, mesh.shape["tp"], mesh.shape["dp"]),
        ("ctx_0", "ctx_1", "tp", "dp"),
    )
    placed = (
        P("dp", CTX, "tp"),
        P("dp", CTX, "tp"),
        P("dp", CTX, "tp"),
        P("tp"),
        P("tp"),
        P(None, "tp"),
        P("tp", CTX_DP),
        P("dp", CTX, "tp"),
        P("dp", None),
    )
    return jax.shard_map(
        per_device,
        mesh=torus,
        in_specs=placed,
        out_specs=(
            P("dp", CTX, "tp"),
            P("dp", CTX, "tp"),
            P("dp", CTX, "tp"),
            P(None, "tp"),
            P(None, "tp"),
        ),
        check_vma=False,
    )
```

profile of v0, /device:TPU:0, one launch (start us, length us, event | category | flops | bytes accessed | tf_op | source)
XLA Modules:
  0.0 960.6 jit_solution(9654145244466244132)
XLA Ops:
  7.9 41.5 %all-gather.11.cloned.1.call-done = bf16[2048,512]{1,0:T(8,128)(2,1)} async-done(((bf16[1024,512]{1,0:T(8,128)(2,1)}), bf16[2048,512]{1,0:T(8,128)(2,1)}) %all-gather.11.cloned.1.call-update) | async-done | bytes 2097168 | tf_op jit(solution)/shard_map/all_gather | solution.py:23
  49.5 60.1 %all-gather.13.cloned.1.call-done = bf16[4,1024,512]{2,1,0:T(8,128)(2,1)} async-done(((bf16[2,1024,512]{2,1,0:T(8,128)(2,1)}), bf16[4,1024,512]{2,1,0:T(8,128)(2,1)}) %all-gather.13.cloned.1.call-update) | async-done | bytes 4194320 | tf_op jit(solution)/shard_map/all_gather | solution.py:23
  112.2 4.3 collective-permute-start.1
  125.9 22.6 %rev.9 = bf16[1024,1024]{0,1:T(8,128)(2,1)} reverse(bf16[1024,1024]{0,1:T(8,128)(2,1)S(1)} %copy.82), dimensions={0} | reverse | bytes 4194304 | tf_op jit(solution)/shard_map/rev | solution.py:132
  150.5 149.7 %all-gather.15.cloned.1.call-done = bf16[8,2,1024,512]{3,2,1,0:T(8,128)(2,1)} async-done(((bf16[2,2,1024,512]{3,2,1,0:T(8,128)(2,1)}), bf16[8,2,1024,512]{3,2,1,0:T(8,128)(2,1)}) %all-gather.15.cloned.1.call-update) | async-done | bytes 16777232 | tf_op jit(solution)/shard_map/all_gather | solution.py:23
  300.2 14.0 %copy.83 = bf16[8,2,1024,512]{3,2,0,1:T(8,128)(2,1)} copy(bf16[8,2,1024,512]{3,2,1,0:T(8,128)(2,1)} %all-gather.15.cloned.1.call-done) | data formatting | bytes 33554432 | tf_op jit(solution)/shard_map/all_gather | solution.py:23
  314.2 21.8 %copy.84 = bf16[1024,16,512]{0,2,1:T(8,128)(2,1)} copy(bf16[1024,16,512]{2,0,1:T(8,128)(2,1)} %bitcast.180) | data formatting | bytes 33554432 | tf_op jit(solution)/shard_map/transpose | solution.py:17
  336.0 12.9 %all-gather.9.cloned.1.call-done = bf16[1,512,8192]{2,1,0:T(8,128)(2,1)} async-done(((bf16[1,512,1024]{2,1,0:T(8,128)(2,1)}), bf16[1,512,8192]{2,1,0:T(8,128)(2,1)}) %all-gather.9.cloned.1.call-update) | async-done | bytes 8388624 | tf_op jit(solution)/shard_map/all_gather | solution.py:110
  348.9 14.8 %fusion.62 = bf16[64,8,8,128]{3,2,1,0:T(8,128)(2,1)S(1)} fusion(bf16[1024,8192]{0,1:T(8,128)(2,1)} %bitcast.181, bf16[1,512,8192]{2,1,0:T(8,128)(2,1)} %all-gather.9.cloned.1.call-done), kind=kOutput, calls=%fused_computation.79 | convolution fusion | flops 8590458880 | bytes 26214400 | tf_op jit(solution)/shard_map/sd,hd->sh/dot_general | solution.py:112
  364.8 388.5 %while.27 = (s32[]{:T(128)}, bf16[8,512,128]{2,1,0:T(8,128)(2,1)}, f32[8,512,128]{2,1,0:T(8,128)}, f32[8,512,128]{2,1,0:T(8,128)}, f32[8,512,128]{2,1,0:T(8,128)...) while((s32[]{:T(128)}, bf16[8,512,128]{2,1,0:T(8,128)(2,1)}, ...), condition=%wide.region_9.10_spmd.clone, body=%wide.region_3.9_spmd.clone.sunk | while | flops 1088420096 | bytes 80905624 | solution.py:167
  381.3 4.0 reshape.174
  395.2 4.9 reshape.175
  404.3 3.5 rev.12
  429.9 4.0 reshape.174
  443.8 4.9 reshape.175
  478.5 4.0 reshape.174
  492.4 4.9 reshape.175
  501.5 3.5 rev.12
  527.0 4.0 reshape.174
  540.9 4.9 reshape.175
  575.6 4.0 reshape.174
  589.5 4.9 reshape.175
  624.2 4.0 reshape.174
  638.0 4.9 reshape.175
  672.7 4.0 reshape.174
  686.6 4.9 reshape.175
  721.3 4.0 reshape.174
  735.2 4.9 reshape.175
  753.4 4.7 copy_bitcast_fusion
  764.1 136.7 %psum.15 = f32[2,1024]{1,0:T(2,128)} all-reduce(f32[2,1024]{1,0:T(2,128)S(1)} %pad_maximum_fusion.3), channel_id=1, replica_groups=mesh['ctx_0'=2,'ctx_1'=4,'tp'=8,'dp'=2] {'ctx_0','ctx_1','dp'}, use_global_device_ids=true, to_apply=%region_11.12 | all-reduce | flops 2048 | bytes 16384 | tf_op jit(solution)/shard_map/psum | solution.py:172
  908.4 40.9 %all-reduce.5.cloned.1.call-done = f32[1024,1024]{1,0:T(8,128)} async-done(((f32[1024,1024]{1,0:T(8,128)}), f32[1024,1024]{1,0:T(8,128)}) %all-reduce.5.cloned.1.call-update) | async-done | bytes 4194320 | tf_op jit(solution)/shard_map/psum | solution.py:172
  949.3 4.8 copy.159
  (398 shorter events, 339.2 us)
Async XLA Ops:
  7.2 42.3 %all-gather.11.cloned.1.call-start = ((), (), s32[]{:S(2)}) async-start(), calls=%async_computation.2 | async-start | bytes 3145728 | tf_op jit(solution)/shard_map/all_gather | solution.py:23
  7.9 101.7 %all-gather.13.cloned.1.call-start = ((), (), s32[]{:S(2)}) async-start(), calls=%async_computation.3 | async-start | bytes 6291456 | tf_op jit(solution)/shard_map/all_gather | solution.py:23
  49.5 250.7 %all-gather.15.cloned.1.call-start = ((), (), s32[]{:S(2)}) async-start(), calls=%async_computation.4 | async-start | bytes 20971520 | tf_op jit(solution)/shard_map/all_gather | solution.py:23
  109.7 6.9 copy-start.7
  109.7 239.2 %all-gather.9.cloned.1.call-start = ((), (), s32[]{:S(2)}) async-start(), calls=%async_computation.1 | async-start | bytes 9437184 | tf_op jit(solution)/shard_map/all_gather | solution.py:110
  110.2 11.0 %copy-start.11 = (s32[1,16]{1,0:T(1,128)S(1)}, s32[1,16]{1,0:T(1,128)}, u32[]{:S(2)}) copy-start(s32[1,16]{1,0:T(1,128)} %param.19) | copy-start | bytes 196
  110.2 11.2 %copy-start.8 = (bf16[1,512,1024]{2,1,0:T(8,128)(2,1)S(1)}, bf16[1,512,1024]{2,1,0:T(8,128)(2,1)}, u32[]{:S(2)}) copy-start(bf16[1,512,1024]{2,1,0:T(8,128)(2,1)} %param.11) | copy-start | bytes 3145732
  110.3 839.0 %all-reduce.5.cloned.1.call-start = ((), (), s32[]{:S(2)}) async-start(), calls=%async_computation | async-start | bytes 8388608 | tf_op jit(solution)/shard_map/psum | solution.py:172
  112.2 252.7 %collective-permute-start.1 = (bf16[512,1024]{0,1:T(8,128)(2,1)}, bf16[512,1024]{0,1:T(8,128)(2,1)}, u32[]{:S(2)}, u32[]{:S(2)}) collective-permute-start(bf16[512,1024]{0,1:T(8,128)(2,1)} %bitcast.20), channel_id=1, source_target_pairs={{0,16},{16,32},{32,48},{48,64},{64,80},{80,96},{96,112},{1,17},{17... | collective-permute-start | bytes 3145736 | tf_op jit(solution)/shard_map/ppermute | solution.py:37
  117.8 247.0 %collective-permute-start = (bf16[512,1024]{0,1:T(8,128)(2,1)}, bf16[512,1024]{0,1:T(8,128)(2,1)}, u32[]{:S(2)}, u32[]{:S(2)}) collective-permute-start(bf16[512,1024]{0,1:T(8,128)(2,1)} %bitcast.3), channel_id=1, source_target_pairs={{0,16},{16,32},{32,48},{48,64},{64,80},{80,96},{96,112},{1,17},{17... | collective-permute-start | bytes 3145736 | tf_op jit(solution)/shard_map/ppermute | solution.py:37
  404.3 8.1 copy-start
  404.3 8.1 copy-start.1
  452.9 8.1 copy-start
  452.9 8.1 copy-start.1
  501.5 8.1 copy-start
  501.5 8.1 copy-start.1
  550.0 8.1 copy-start
  550.0 8.1 copy-start.1
  598.6 8.1 copy-start
  598.6 8.1 copy-start.1
  630.4 2.6 copy-start.2
  647.2 8.1 copy-start
  647.2 8.1 copy-start.1
  695.7 8.1 copy-start
  695.7 8.1 copy-start.1
  744.3 8.1 copy-start
  744.3 8.1 copy-start.1
  758.2 142.6 %collective-permute-start.2 = (f32[8,512,128]{2,1,0:T(8,128)}, f32[8,512,128]{2,1,0:T(8,128)}, u32[]{:S(2)}, u32[]{:S(2)}) collective-permute-start(f32[8,512,128]{2,1,0:T(8,128)} %get-tuple-element.248), channel_id=1, source_target_pairs={{16,0},{32,16},{48,32},{64,48},{80,64},{96,80},{112,96},{17,1},{33... | collective-permute-start | bytes 6291464 | tf_op jit(solution)/shard_map/ppermute | solution.py:37
  759.5 145.1 %collective-permute-start.3 = (f32[8,512,128]{2,1,0:T(8,128)}, f32[8,512,128]{2,1,0:T(8,128)}, u32[]{:S(2)}, u32[]{:S(2)}) collective-permute-start(f32[8,512,128]{2,1,0:T(8,128)} %get-tuple-element.250), channel_id=1, source_target_pairs={{16,0},{32,16},{48,32},{64,48},{80,64},{96,80},{112,96},{17,1},{33... | collective-permute-start | bytes 6291464 | tf_op jit(solution)/shard_map/ppermute | solution.py:37
  760.8 3.4 copy-start.9
  760.8 3.4 copy-start.10
  760.8 140.0 %copy-start.5 = (f32[8,512,128]{2,1,0:T(8,128)S(1)}, f32[8,512,128]{2,1,0:T(8,128)}, u32[]{:S(2)}) copy-start(f32[8,512,128]{2,1,0:T(8,128)} %get-tuple-element.247) | copy-start | bytes 6291460
  (17 other events, 41.6 us)
Sparse Core Ops, SparseCore 0:
  9.6 39.7 all-gather.10
  51.1 58.4 all-gather.12
  111.3 188.8 all-gather.14
  301.7 47.1 all-gather.8
  758.3 190.9 all-reduce.4
where the time goes:
time: 967 us; the launch traced here: 961 us
  local copies, waits for them, and re-layouts  351 us (36%)
  waiting for transfers between devices  306 us (32%)
  blocking collectives  137 us (14%)
  matrix products  125 us (13%)
  other arithmetic  15.6 us (2%)
  between operations  13.9 us (1%)
  starting transfers between devices  10.5 us (1%)
    all_gather x3, waiting for transfers between devices, stacked_from(): blocks = lax.all_gather(blocks, axes[k])  251 us
    psum x1, blocking collectives, per_device(): lax.psum((from_heads(grad_rel), bias_terms), CTX_DP)  137 us
    dynamic_slice x80, local copies, waits for them, and re-layouts, per_device(): lax.map(per_head, stacked)  51.6 us
    psum x1, waiting for transfers between devices, per_device(): lax.psum((from_heads(grad_rel), bias_terms), CTX_DP)  40.9 us
    reshape x8, local copies, waits for them, and re-layouts, unskew_rows(): return flattened.reshape(seg_len, 4 * seg_len + 1)[:, :2 * seg_len]  39.1 us
    dynamic_update_slice x32, local copies, waits for them, and re-layouts, per_device(): lax.map(per_head, stacked)  35 us
    reshape x8, local copies, waits for them, and re-layouts, skew_rows(): return window.reshape(seg_len, 3 * seg_len - 1)[:, :2 * seg_len]  31.8 us
    rev x8, local copies, waits for them, and re-layouts, head_backward(): jnp.einsum('ie,id->ed', grad_shifted, query_position, preferred_element_t...  28.1 us
  transfers between devices with their start and end apart: 9, of which 5 were waited for; matrix products, arithmetic and copies ran while one was open for 10% of the time, Pallas kernels for 0%

commit v1 on v0

v1 whole, which is shorter than its diff:
```python
import functools
import math

import jax
import jax.numpy as jnp
from jax import lax
from jax.experimental import pallas as pl
from jax.experimental.pallas import tpu as pltpu
from jax.sharding import Mesh
from jax.sharding import PartitionSpec as P

HD = 128
SCALE = 1.0 / math.sqrt(HD)


def dot_nt(a, b):
    return lax.dot_general(a, b, (((1,), (1,)), ((), ())), preferred_element_type=jnp.float32)


def dot_nn(a, b):
    return lax.dot_general(a, b, (((1,), (0,)), ((), ())), preferred_element_type=jnp.float32)


def dot_tn(a, b):
    return lax.dot_general(a, b, (((0,), (0,)), ((), ())), preferred_element_type=jnp.float32)


def exchange(block=256):
    i = lax.broadcasted_iota(jnp.int32, (block, block), 0)
    j = lax.broadcasted_iota(jnp.int32, (block, block), 1)
    return jnp.where(i + j == block - 1, 1.0, 0.0).astype(jnp.bfloat16)


def flipped_lanes(x, anti):
    block = anti.shape[0]
    n = x.shape[1] // block
    parts = [dot_nn(x[:, k * block:(k + 1) * block], anti) for k in range(n)]
    return jnp.concatenate(parts[::-1], axis=1)


def flipped(rows, block=256):
    n = rows.shape[0] // block
    anti = exchange(block)
    parts = [dot_nn(anti, rows[k * block:(k + 1) * block]) for k in range(n)]
    return jnp.concatenate(parts[::-1], axis=0).astype(jnp.bfloat16)


def weights_body(start, q, k_mem, k_own, rel, bu, bw, w_out, *, block):
    seg = q.shape[0]
    rel_back = flipped(rel[...])
    q32 = q[...].astype(jnp.float32)
    qc = (q32 + bu[...]).astype(jnp.bfloat16)
    qp = (q32 + bw[...]).astype(jnp.bfloat16)
    for r in range(seg // block):
        rows = slice(r * block, (r + 1) * block)
        own = (r + 1) * block
        width = seg + own
        content = jnp.concatenate(
            [dot_nt(qc[rows], k_mem[...]), dot_nt(qc[rows], k_own[:own])], axis=1)
        raw = dot_nt(qp[rows], rel_back[seg - own:])
        raw = pltpu.roll(raw, width - block + 1, 1, stride=1, stride_axis=0)
        col = lax.broadcasted_iota(jnp.int32, (block, width), 1)
        row = lax.broadcasted_iota(jnp.int32, (block, 1), 0)
        seen = (col >= start[rows]) & (col <= row + (r * block + seg))
        logits = jnp.where(seen, (content + raw) * SCALE, -jnp.inf)
        peak = jnp.max(logits, axis=1, keepdims=True)
        raised = jnp.exp(logits - peak)
        w_out[0, rows, :width] = raised / jnp.sum(raised, axis=1, keepdims=True)


def grads_body(w, g, q, k_mem, k_own, v_mem, v_own, rel, bu, bw,
               dq_out, dk_mem, dk_own, dv_mem, dv_own, drel_out, bias_out,
               dk_acc, dv_acc, dr_acc, *, block):
    seg = q.shape[0]
    q32 = q[...].astype(jnp.float32)
    qc = (q32 + bu[...]).astype(jnp.bfloat16)
    qp = (q32 + bw[...]).astype(jnp.bfloat16)
    sum_u = sum_w = 0.0
    nblk = seg // block
    anti = exchange()
    for r in reversed(range(nblk)):
        rows = slice(r * block, (r + 1) * block)
        own = (r + 1) * block
        width = seg + own
        dw = jnp.concatenate(
            [dot_nt(g[rows], v_mem[...]), dot_nt(g[rows], v_own[:own])], axis=1)
        wr = w[0, rows, :width]
        inner = jnp.sum(wr * dw, axis=1, keepdims=True)
        gl32 = wr * (dw - inner) * SCALE
        gl = gl32.astype(jnp.bfloat16)
        gs = pltpu.roll(flipped_lanes(gl, anti), width - block + 1, 1, stride=1, stride_axis=0)
        gs = gs.astype(jnp.bfloat16)
        wl = wr.astype(jnp.bfloat16)
        part_u = dot_nn(gl[:, :seg], k_mem[...]) + dot_nn(gl[:, seg:], k_own[:own])
        part_w = dot_nn(gs, rel[:width])
        dq_out[rows] = (part_u + part_w).astype(jnp.bfloat16)
        sum_u = sum_u + jnp.sum(part_u, axis=0, keepdims=True)
        sum_w = sum_w + jnp.sum(part_w, axis=0, keepdims=True)
        dk = dot_tn(gl, qc[rows])
        dv = dot_tn(wl, g[rows])
        dr = dot_tn(gs, qp[rows])
        if r == nblk - 1:
            dk_acc[...] = dk
            dv_acc[...] = dv
            dr_acc[...] = dr
        else:
            dk_acc[:width] = dk_acc[:width] + dk
            dv_acc[:width] = dv_acc[:width] + dv
            dr_acc[:width] = dr_acc[:width] + dr
    dk_mem[...] = dk_acc[:seg].astype(dk_mem.dtype)
    dk_own[...] = dk_acc[seg:]
    dv_mem[...] = dv_acc[:seg].astype(dv_mem.dtype)
    dv_own[...] = dv_acc[seg:]
    drel_out[...] = dr_acc[...].astype(jnp.bfloat16)
    bias_out[0:1, :] = sum_u
    bias_out[1:2, :] = sum_w


def weights_call(start, q, k_mem, k_own, rel, bu, bw, h0=0, heads=8, block=256):
    seg = q.shape[0]
    rels = rel.shape[0]
    col = lambda n: pl.BlockSpec((n, HD), lambda h: (0, h + h0))
    out = lambda n: pl.BlockSpec((n, HD), lambda h: (0, h))
    return pl.pallas_call(
        functools.partial(weights_body, block=block),
        grid=(heads,),
        in_specs=[pl.BlockSpec((seg, 1), lambda h: (0, 0)), col(seg), col(seg), col(seg), col(rels), col(1), col(1)],
        out_specs=pl.BlockSpec((1, seg, 2 * seg), lambda h: (h, 0, 0)),
        out_shape=jax.ShapeDtypeStruct((heads, seg, 2 * seg), jnp.float32),
        name="attn_weights",
    )(start, q, k_mem, k_own, rel, bu, bw)


def grads_call(w, g, q, k_mem, k_own, v_mem, v_own, rel, bu, bw, h0=0, heads=8, block=256):
    seg = q.shape[0]
    rels = rel.shape[0]
    col = lambda n: pl.BlockSpec((n, HD), lambda h: (0, h + h0))
    out = lambda n: pl.BlockSpec((n, HD), lambda h: (0, h))
    f = lambda n, dt: jax.ShapeDtypeStruct((n, heads * HD), dt)
    bf, f32 = jnp.bfloat16, jnp.float32
    return pl.pallas_call(
        functools.partial(grads_body, block=block),
        grid=(heads,),
        in_specs=[pl.BlockSpec((1, seg, 2 * seg), lambda h: (h + h0, 0, 0)), out(seg), col(seg), col(seg), col(seg),
                  col(seg), col(seg), col(rels), col(1), col(1)],
        out_specs=[out(seg)] * 5 + [out(rels), out(2)],
        out_shape=[f(seg, bf), f(seg, bf), f(seg, f32), f(seg, bf), f(seg, f32), f(rels, bf), f(2, f32)],
        scratch_shapes=[pltpu.VMEM((rels, HD), f32)] * 3,
        name="attn_grads",
    )(w, g, q, k_mem, k_own, v_mem, v_own, rel, bu, bw)


AXES = ("zh", "x", "y", "co", "zl")
CTX = ("zh", "x")
Z = ("zh", "zl")
TP = ("y", "co")
CTX_DP = ("zh", "x", "zl")
NEAR = (0, -1, 1, 2)


def hop(value, axis, steps):
    count = lax.axis_size(axis)
    return lax.ppermute(value, axis, [(i, (i + steps) % count) for i in range(count)])


def from_behind(value, axis, steps):
    count = lax.axis_size(axis)
    first, last = (max(0, -steps), min(count, count - steps))
    return lax.ppermute(value, axis, [(i, i + steps) for i in range(first, last)])


def ring_gather(own, axis):
    half = own.shape[0] // 2
    behind = hop(own, axis, 1)
    ahead = hop(own, axis, -1)
    return behind, ahead, hop(behind[:half], axis, 1), hop(ahead[half:], axis, -1)


def stacked_ring(own, axis):
    behind, ahead, far_low, far_high = ring_gather(own, axis)
    return jnp.stack([own, behind, ahead, jnp.concatenate([far_low, far_high], axis=0)])


def two_axes(own, first, second):
    near = stacked_ring(own, first)
    return (near,) + ring_gather(near, second)


def project_body(slices, blocks, w0, w1, w2, w3, w4, cot_own, cot_side, out, cot, wbuf, acc, cot_sem, w_sem):
    parts = [(ref, i) for ref in (w0, w1, w2, w3, w4) for i in range(ref.shape[0])]
    depth = wbuf.shape[0]
    wide = cot.shape[2]

    def w_copy(k):
        ref, i = parts[k]
        return pltpu.make_async_copy(ref.at[i], wbuf.at[k % depth], w_sem.at[k % depth])

    for k in range(depth - 1):
        w_copy(k).start()
    cot_copies = []
    for side, ref in enumerate((cot_own, cot_side)):
        for i in range(ref.shape[0]):
            for part in range(2):
                block = blocks[side * ref.shape[0] + i] * 2 + part
                cot_copies.append(pltpu.make_async_copy(
                    ref.at[i, :, pl.ds(part * wide, wide)], cot.at[block], cot_sem.at[side, i, part]))
    for copy in cot_copies:
        copy.start()
    for copy in cot_copies:
        copy.wait()
    for k in range(len(parts)):
        if k + depth - 1 < len(parts):
            w_copy(k + depth - 1).start()
        w_copy(k).wait()
        product = dot_nt(cot[slices[k]], wbuf[k % depth])
        if k == 0:
            acc[...] = product
        elif k < len(parts) - 1:
            acc[...] = acc[...] + product
        else:
            out[...] = (acc[...] + product).astype(out.dtype)


def project(slices, blocks, pieces, cot_own, cot_side):
    rows, depth = pieces[0].shape[1:]
    tokens = cot_own.shape[1]
    return pl.pallas_call(
        project_body,
        in_specs=[pl.BlockSpec(memory_space=pltpu.SMEM)] * 2 + [pl.BlockSpec(memory_space=pl.ANY)] * 7,
        out_shape=jax.ShapeDtypeStruct((tokens, rows), jnp.bfloat16),
        scratch_shapes=[
            pltpu.VMEM((16, tokens, depth), jnp.bfloat16),
            pltpu.VMEM((4, rows, depth), jnp.bfloat16),
            pltpu.VMEM((tokens, rows), jnp.float32),
            pltpu.SemaphoreType.DMA((2, 4, 2)),
            pltpu.SemaphoreType.DMA((4,)),
        ],
        cost_estimate=pl.CostEstimate(
            flops=2 * tokens * rows * depth * 16, bytes_accessed=2 * (16 * rows * depth + 16 * tokens * depth),
            transcendentals=0),
        name="project",
    )(slices, blocks, *pieces, cot_own, cot_side)


def block_of(value, index, count):
    rows = value.shape[0] // count
    return lax.dynamic_slice_in_dim(value, (index % count) * rows, rows, 0)


def scatter_sum(value, axis):
    here = lax.axis_index(axis)
    own = block_of(value, here, 4).astype(jnp.float32)
    got = [hop(block_of(value, here + k, 4), axis, k).astype(jnp.float32) for k in (1, 3, 2)]
    return ((own + got[2]) + (got[0] + got[1])).astype(value.dtype)


def gather_rows(block, axis):
    here = lax.axis_index(axis)
    rows = block.shape[0]
    got = [hop(block, axis, k) for k in (1, 3, 2)]
    out = jnp.zeros((4 * rows,) + block.shape[1:], block.dtype)
    for k, piece in zip((0, 1, 3, 2), [block] + got):
        out = lax.dynamic_update_slice_in_dim(out, piece, ((here - k) % 4) * rows, 0)
    return out


def summed_rows(value, first, second):
    part = scatter_sum(scatter_sum(value, first), second)
    return gather_rows(gather_rows(part, second), first)


def summed_small(value):
    for axis in ("x", Z):
        value = (value + hop(value, axis, 2)) + (hop(value, axis, 1) + hop(value, axis, -1))
    return value


def per_device(queries, keys, values, bias_u, bias_w, rel_table, out_weight, grad_out, doc_lengths):
    seg_len = queries.shape[1]
    half = out_weight.shape[0] // 2
    x, y, co, z = (lax.axis_index(a) for a in ("x", "y", "co", Z))
    memory_keys, memory_values = from_behind((keys[0], values[0]), CTX, 1)
    pieces_a = two_axes(out_weight[:half], "x", Z)
    pieces_b = two_axes(out_weight[half:], Z, "x")
    pieces_a = (pieces_a[0],) + pieces_a[1:]
    cot_own = stacked_ring(grad_out[0], "y")
    cot_side = lax.ppermute(cot_own, "co", [(0, 1), (1, 0)])

    def slice_of(dx, dz):
        px, pz = (x + dx) % 4, (z + dz) % 4
        return ((pz // 2) * 4 + px) * 2 + pz % 2

    ids_a = jnp.stack([slice_of(dx, dz) for dz in NEAR for dx in NEAR]).astype(jnp.int32)
    ids_b = jnp.stack([slice_of(dx, dz) for dx in NEAR for dz in NEAR]).astype(jnp.int32)
    blocks = jnp.stack([2 * ((y + dy) % 4) + c for c in (co, 1 - co) for dy in NEAR]).astype(jnp.int32)

    doc_ends = jnp.cumsum(doc_lengths[0])
    seg_start = lax.axis_index(CTX) * seg_len
    token = seg_start + jnp.arange(seg_len, dtype=jnp.int32)
    doc_start = jnp.sum(jnp.where(doc_ends[None, :] <= token[:, None], doc_lengths[0][None, :], 0), axis=1)
    start = (doc_start - (seg_start - seg_len)).astype(jnp.int32)[:, None]

    row_u, row_w = bias_u[None, :], bias_w[None, :]
    weights = weights_call(start, queries[0], memory_keys, keys[0], rel_table, row_u, row_w)
    outs = []
    for ids, pieces, first in ((ids_a, pieces_a, 0), (ids_b, pieces_b, 4)):
        grad_heads = project(ids, blocks, pieces, cot_own, cot_side)
        outs.append(grads_call(
            weights, grad_heads, queries[0], memory_keys, keys[0], memory_values, values[0],
            rel_table, row_u, row_w, h0=first, heads=4))
    done = []
    for part, (dq, dk_mem, dk_own, dv_mem, dv_own, table, biases) in enumerate(outs):
        back_keys, back_values = from_behind((dk_mem, dv_mem), CTX, -1)
        grad_keys = (dk_own + back_keys.astype(jnp.float32)).astype(jnp.bfloat16)
        grad_values = (dv_own + back_values.astype(jnp.float32)).astype(jnp.bfloat16)
        order = ("x", Z) if part == 0 else (Z, "x")
        grad_table = summed_rows(table, *order).astype(jnp.float32)
        done.append((dq, grad_keys, grad_values, grad_table, biases))
    dq, grad_keys, grad_values, grad_table, biases = (jnp.concatenate(pair, axis=1) for pair in zip(*done))
    return (dq[None], grad_keys[None], grad_values[None], grad_table, summed_small(biases))


def solution(mesh):
    torus = Mesh(mesh.devices.reshape(2, 4, 4, 2, 2), AXES)
    rows = P("zl", CTX, TP)
    placed = (rows, rows, rows, P(TP), P(TP), P(None, TP), P(TP, CTX_DP), rows, P("zl", None))
    return jax.shard_map(
        per_device,
        mesh=torus,
        in_specs=placed,
        out_specs=(rows, rows, rows, P(None, TP), P(None, TP)),
        check_vma=False,
    )
```

time: 967 us -> 398 us (0.41)
  local copies, waits for them, and re-layouts: 351 us -> 11.7 us
  blocking collectives: 137 us -> 0 us
  matrix products: 125 us -> 0 us
  waiting for transfers between devices: 306 us -> 194 us
  starting transfers between devices: 10.5 us -> 104 us
  Pallas kernels: 0 us -> 65.8 us
  between operations: 13.9 us -> 2.25 us
    all_gather x4 -> x0, waiting for transfers between devices: 264 us -> none  [the longest x3 251 us: stacked_from(): blocks = lax.all_gather(blocks, axes[k])]
    ppermute x4 -> x57, waiting for transfers between devices: 0.01 us -> 194 us  [the longest x50 182 us: hop(): lax.ppermute(value, axis, [(i, (i + steps) % count) for i in range(count)])]
    psum x1 -> x0, blocking collectives: 137 us -> none  [per_device(): lax.psum((from_heads(grad_rel), bias_terms), CTX_DP)]
    dot_general x65 -> x0, matrix products: 125 us -> none  [the longest x8 20.4 us: head_backward(): jnp.einsum('ij,id->jd', weights_low, grad_rows, preferred_element_type=jn...]
    reshape x26 -> x0, local copies, waits for them, and re-layouts: 98 us -> none  [the longest x8 39.1 us: unskew_rows(): return flattened.reshape(seg_len, 4 * seg_len + 1)[:, :2 * seg_len]]
    ppermute x4 -> x57, starting transfers between devices: 10.3 us -> 104 us  [the longest x50 90.1 us: hop(): lax.ppermute(value, axis, [(i, (i + steps) % count) for i in range(count)])]
    pallas_call x0 -> x5, Pallas kernels: none -> 65.8 us  [the longest x2 25.4 us: grads_call(): pl.pallas_call(functools.partial(grads_body, block=block), grid=(heads,),...]
    rev x9 -> x0, local copies, waits for them, and re-layouts: 50.7 us -> none  [the longest x8 28.1 us: head_backward(): jnp.einsum('ie,id->ed', grad_shifted, query_position, preferred_element_t...]
  transfers between devices with their start and end apart: 9 -> 57, of which waited for: 5 -> 20; matrix products, arithmetic and copies ran while one was open for 10% -> 5% of each run, Pallas kernels for 0% -> 11%
where the time goes in v1:
time: 398 us; the launch traced here: 390 us
  waiting for transfers between devices  194 us (49%)
  starting transfers between devices  104 us (26%)
  Pallas kernels  65.8 us (17%)
  other arithmetic  12.8 us (3%)
  local copies, waits for them, and re-layouts  11.7 us (3%)
    ppermute x50, waiting for transfers between devices, hop(): lax.ppermute(value, axis, [(i, (i + steps) % count) for i in range(count)])  182 us
    ppermute x50, starting transfers between devices, hop(): lax.ppermute(value, axis, [(i, (i + steps) % count) for i in range(count)])  90.1 us
    pallas_call x2, Pallas kernels, grads_call(): pl.pallas_call(functools.partial(grads_body, block=block), grid=(heads,),...  25.4 us
    pallas_call x2, Pallas kernels, project(): pl.pallas_call(project_body, in_specs=[pl.BlockSpec(memory_space=pltpu.SM...  22.5 us
    pallas_call x1, Pallas kernels, weights_call(): pl.pallas_call(functools.partial(weights_body, block=block), grid=(heads,...  18 us
    ppermute x6, starting transfers between devices, from_behind(): lax.ppermute(value, axis, [(i, i + steps) for i in range(first, last)])  13.5 us
    ppermute x6, waiting for transfers between devices, from_behind(): lax.ppermute(value, axis, [(i, i + steps) for i in range(first, last)])  12.1 us
  transfers between devices with their start and end apart: 57, of which 20 were waited for; matrix products, arithmetic and copies ran while one was open for 5% of the time, Pallas kernels for 11%

profile of v1, /device:TPU:0, one launch (start us, length us, event | category | flops | bytes accessed | tf_op | source)
XLA Modules:
  0.0 390.1 jit_solution(5475481021044054913)
XLA Ops:
  0.6 3.2 collective-permute-start.10
  8.5 18.1 %collective-permute-done.10 = bf16[512,1024]{1,0:T(8,128)(2,1)S(1)} collective-permute-done((bf16[512,1024]{1,0:T(8,128)(2,1)}, bf16[512,1024]{1,0:T(8,128)(2,1)S(1)}, u32[]{:S(2)}, u32[]{:S(2)}) %collective-permute-start.10) | collective-permute-done | bytes 1048608 | tf_op jit(solution)/shard_map/ppermute | solution.py:163
  26.6 3.7 collective-permute-start.12
  36.2 4.4 %collective-permute-done.12 = bf16[256,1024]{1,0:T(8,128)(2,1)S(1)} collective-permute-done((bf16[256,1024]{1,0:T(8,128)(2,1)S(1)}, bf16[256,1024]{1,0:T(8,128)(2,1)S(1)}, u32[]{:S(2)}, u32[]{:S(2)}) %collective-permute-start.12) | collective-permute-done | bytes 524320 | tf_op jit(solution)/shard_map/ppermute | solution.py:163
  53.2 4.6 %collective-permute-done.17 = bf16[256,512]{1,0:T(8,128)(2,1)S(1)} collective-permute-done((bf16[256,512]{1,0:T(8,128)(2,1)S(1)}, bf16[256,512]{1,0:T(8,128)(2,1)S(1)}, u32[]{:S(2)}, u32[]{:S(2)}) %collective-permute-start.17) | collective-permute-done | bytes 262176 | tf_op jit(solution)/shard_map/ppermute | solution.py:163
  61.0 41.2 %collective-permute-done.6.w2 = bf16[4,512,512]{2,1,0:T(8,128)(2,1)S(1)} collective-permute-done((bf16[4,512,512]{2,1,0:T(8,128)(2,1)S(1)}, bf16[4,512,512]{2,1,0:T(8,128)(2,1)S(1)}, u32[]{:S(2)}, u32[]{:S(2)}) %collective-permute-start.6) | collective-permute-done | bytes 2097184 | tf_op jit(solution)/shard_map/ppermute | solution.py:163
  102.2 3.7 collective-permute-start
  106.0 3.5 collective-permute-start.8
  110.6 4.5 %collective-permute-start.14 = (bf16[512,1024]{1,0:T(8,128)(2,1)S(1)}, bf16[512,1024]{1,0:T(8,128)(2,1)}, u32[]{:S(2)}, u32[]{:S(2)}) collective-permute-start(bf16[512,1024]{1,0:T(8,128)(2,1)S(1)} %bitcast.64), channel_id=1, source_target_pairs={{0,16},{16,32},{32,48},{48,64},{64,80},{80,96},{96,112},{1,17},{17... | collective-permute-start | bytes 3145736 | tf_op jit(solution)/shard_map/ppermute | solution.py:169
  117.2 12.1 %collective-permute-done.k_mem = bf16[512,1024]{1,0:T(8,128)(2,1)S(1)} collective-permute-done((bf16[512,1024]{1,0:T(8,128)(2,1)S(1)}, bf16[512,1024]{1,0:T(8,128)(2,1)S(1)}, u32[]{:S(2)}, u32[]{:S(2)}) %collective-permute-start) | collective-permute-done | bytes 1048608 | tf_op jit(solution)/shard_map/ppermute | solution.py:169
  129.4 4.6 %collective-permute-start.22 = (bf16[2,512,512]{2,1,0:T(8,128)(2,1)}, bf16[2,512,512]{2,1,0:T(8,128)(2,1)S(1)}, u32[]{:S(2)}, u32[]{:S(2)}) collective-permute-start(bf16[2,512,512]{2,1,0:T(8,128)(2,1)} %slice.57), channel_id=1, source_target_pairs={{0,48},{16,0},{32,16},{48,32},{1,49},{17,1},{33,17},{49,33},{2,50}... | collective-permute-start | bytes 3145736 | tf_op jit(solution)/shard_map/ppermute | solution.py:163
  134.0 42.4 %collective-permute-done.8.w4 = bf16[2,512,512]{2,1,0:T(8,128)(2,1)} collective-permute-done((bf16[2,512,512]{2,1,0:T(8,128)(2,1)S(1)}, bf16[2,512,512]{2,1,0:T(8,128)(2,1)}, u32[]{:S(2)}, u32[]{:S(2)}) %collective-permute-start.8) | collective-permute-done | bytes 1048608 | tf_op jit(solution)/shard_map/ppermute | solution.py:163
  180.1 18.0 %attn_weights.1.w = f32[8,512,1024]{2,1,0:T(8,128)} custom-call(s32[512,1]{1,0:T(8,128)} %copy.18.start, bf16[512,1024]{1,0:T(8,128)(2,1)} %bitcast.55, bf16[512,1024]{1,0:T(8,128)(2,1)} %copy-done.1, bf16[512,1024]{1,0:T(8,128)(2,1)} %bitcast.58, bf16[1024,1024]{1,0:T(8,128)(2,1)} %rel.5, f32[1,1024]{1,0:T(1,128)} %bitcast.73, f32[1,1024]{1,0:T(1,128)} %bitcast.76), custom_call_target="tpu_custom_call" | custom-call | tf_op jit(solution)/shard_map/attn_weights/pallas_call | solution.py:124
  198.1 11.2 %project.2.g = bf16[512,512]{1,0:T(8,128)(2,1)} custom-call(s32[16]{0:T(128)} %stack.155.slices, s32[8]{0:T(128)} %stack.164.blocks, bf16[4,512,512]{2,1,0:T(8,128)(2,1)} %copy-done.3, bf16[4,512,512]{2,1,0:T(8,128)(2,1)} %copy-done.7, bf16[4,512,512]{2,1,0:T(8,128)(2,1)} %copy-done.6, bf16[2,512,512]{2,1,0:T(8,128)(2,1)} %collective-permute-done.7.w3, ...), custom_call_target="tpu_custom_call" | custom-call | flops 4294967296 | bytes 16777216 | tf_op jit(solution)/shard_map/project/pallas_call | solution.py:227
  209.3 12.6 %attn_grads.2 = (bf16[512,512]{1,0:T(8,128)(2,1)}, bf16[512,512]{1,0:T(8,128)(2,1)}, f32[512,512]{1,0:T(8,128)}, bf16[512,512]{1,0:T(8,128)(2,1)}, f32[512,512]{...) custom-call(f32[8,512,1024]{2,1,0:T(8,128)} %attn_weights.1.w, bf16[512,512]{1,0:T(8,128)(2,1)} %project.2.g, ...), custom_call_target="tpu_custom_call" | custom-call | tf_op jit(solution)/shard_map/attn_grads/pallas_call | solution.py:141
  223.6 11.3 %project.3.g = bf16[512,512]{1,0:T(8,128)(2,1)} custom-call(s32[16]{0:T(128)} %stack.174.slices, s32[8]{0:T(128)} %stack.164.blocks, bf16[4,512,512]{2,1,0:T(8,128)(2,1)} %copy-done.2, bf16[4,512,512]{2,1,0:T(8,128)(2,1)} %copy-done.5, bf16[4,512,512]{2,1,0:T(8,128)(2,1)} %copy-done.4, bf16[2,512,512]{2,1,0:T(8,128)(2,1)} %collective-permute-done.21.w3, ...), custom_call_target="tpu_custom_call" | custom-call | flops 4294967296 | bytes 16777216 | tf_op jit(solution)/shard_map/project/pallas_call | solution.py:227
  234.8 12.8 %attn_grads.3 = (bf16[512,512]{1,0:T(8,128)(2,1)}, bf16[512,512]{1,0:T(8,128)(2,1)}, f32[512,512]{1,0:T(8,128)}, bf16[512,512]{1,0:T(8,128)(2,1)}, f32[512,512]{...) custom-call(f32[8,512,1024]{2,1,0:T(8,128)} %attn_weights.1.w, bf16[512,512]{1,0:T(8,128)(2,1)} %project.3.g, ...), custom_call_target="tpu_custom_call" | custom-call | tf_op jit(solution)/shard_map/attn_grads/pallas_call | solution.py:141
  253.9 3.9 %collective-permute-start.41 = (bf16[256,512]{1,0:T(8,128)(2,1)S(1)}, bf16[256,512]{1,0:T(8,128)(2,1)S(1)}, u32[]{:S(2)}, u32[]{:S(2)}) collective-permute-start(bf16[256,512]{1,0:T(8,128)(2,1)S(1)} %get-tuple-element.41), channel_id=1, source_target_pairs={{0,65},{1,0},{64,1},{65,64},{2,67},{3,2},{66,3},{67,66},{4,69},{5,... | collective-permute-start | bytes 786440 | tf_op jit(solution)/shard_map/ppermute | solution.py:163
  263.3 5.4 %collective-permute-done.56 = f32[2,1024]{1,0:T(2,128)S(1)} collective-permute-done((f32[2,1024]{1,0:T(2,128)S(1)}, f32[2,1024]{1,0:T(2,128)S(1)}, u32[]{:S(2)}, u32[]{:S(2)}) %collective-permute-start.56) | collective-permute-done | bytes 8224 | tf_op jit(solution)/shard_map/ppermute | solution.py:163
  275.8 5.0 %collective-permute-start.27 = (bf16[256,512]{1,0:T(8,128)(2,1)S(1)}, bf16[256,512]{1,0:T(8,128)(2,1)S(1)}, u32[]{:S(2)}, u32[]{:S(2)}) collective-permute-start(bf16[256,512]{1,0:T(8,128)(2,1)S(1)} %get-tuple-element.37), channel_id=1, source_target_pairs={{0,32},{16,48},{32,0},{48,16},{1,33},{17,49},{33,1},{49,17},{2,34}... | collective-permute-start | bytes 786440 | tf_op jit(solution)/shard_map/ppermute | solution.py:163
  284.0 4.0 %collective-permute-done.27 = bf16[256,512]{1,0:T(8,128)(2,1)S(1)} collective-permute-done((bf16[256,512]{1,0:T(8,128)(2,1)S(1)}, bf16[256,512]{1,0:T(8,128)(2,1)S(1)}, u32[]{:S(2)}, u32[]{:S(2)}) %collective-permute-start.27) | collective-permute-done | bytes 262176 | tf_op jit(solution)/shard_map/ppermute | solution.py:163
  288.0 3.3 collective-permute-start.42
  291.2 16.5 %collective-permute-done.29 = bf16[256,512]{1,0:T(8,128)(2,1)S(1)} collective-permute-done((bf16[256,512]{1,0:T(8,128)(2,1)S(1)}, bf16[256,512]{1,0:T(8,128)(2,1)S(1)}, u32[]{:S(2)}, u32[]{:S(2)}) %collective-permute-start.29) | collective-permute-done | bytes 262176 | tf_op jit(solution)/shard_map/ppermute | solution.py:163
  310.0 3.0 collective-permute-start.30
  312.9 5.4 %collective-permute-start.32 = (bf16[64,512]{1,0:T(8,128)(2,1)S(1)}, bf16[64,512]{1,0:T(8,128)(2,1)S(1)}, u32[]{:S(2)}, u32[]{:S(2)}) collective-permute-start(bf16[64,512]{1,0:T(8,128)(2,1)S(1)} %get-tuple-element.48), channel_id=1, source_target_pairs={{0,65},{1,0},{64,1},{65,64},{2,67},{3,2},{66,3},{67,66},{4,69},{5,... | collective-permute-start | bytes 196616 | tf_op jit(solution)/shard_map/ppermute | solution.py:163
  324.6 5.0 %collective-permute-done.45 = bf16[64,512]{1,0:T(8,128)(2,1)S(1)} collective-permute-done((bf16[64,512]{1,0:T(8,128)(2,1)S(1)}, bf16[64,512]{1,0:T(8,128)(2,1)S(1)}, u32[]{:S(2)}, u32[]{:S(2)}) %collective-permute-start.45) | collective-permute-done | bytes 65568 | tf_op jit(solution)/shard_map/ppermute | solution.py:163
  331.7 13.4 %collective-permute-done.46 = bf16[64,512]{1,0:T(8,128)(2,1)S(1)} collective-permute-done((bf16[64,512]{1,0:T(8,128)(2,1)S(1)}, bf16[64,512]{1,0:T(8,128)(2,1)S(1)}, u32[]{:S(2)}, u32[]{:S(2)}) %collective-permute-start.46) | collective-permute-done | bytes 65568 | tf_op jit(solution)/shard_map/ppermute | solution.py:163
  345.1 3.0 collective-permute-start.47
  352.2 4.1 %collective-permute-done.33 = bf16[64,512]{1,0:T(8,128)(2,1)S(1)} collective-permute-done((bf16[64,512]{1,0:T(8,128)(2,1)S(1)}, bf16[64,512]{1,0:T(8,128)(2,1)S(1)}, u32[]{:S(2)}, u32[]{:S(2)}) %collective-permute-start.33) | collective-permute-done | bytes 65568 | tf_op jit(solution)/shard_map/ppermute | solution.py:163
  363.1 3.9 %collective-permute-done.35 = bf16[64,512]{1,0:T(8,128)(2,1)S(1)} collective-permute-done((bf16[64,512]{1,0:T(8,128)(2,1)S(1)}, bf16[64,512]{1,0:T(8,128)(2,1)S(1)}, u32[]{:S(2)}, u32[]{:S(2)}) %collective-permute-start.35) | collective-permute-done | bytes 65568 | tf_op jit(solution)/shard_map/ppermute | solution.py:163
  367.0 2.8 collective-permute-start.50
  379.9 7.1 %collective-permute-done.36 = bf16[256,512]{1,0:T(8,128)(2,1)S(1)} collective-permute-done((bf16[256,512]{1,0:T(8,128)(2,1)S(1)}, bf16[256,512]{1,0:T(8,128)(2,1)S(1)}, u32[]{:S(2)}, u32[]{:S(2)}) %collective-permute-start.36) | collective-permute-done | bytes 262176 | tf_op jit(solution)/shard_map/ppermute | solution.py:163
  (196 shorter events, 90.2 us)
Async XLA Ops:
  0.6 25.9 %collective-permute-start.10 = (bf16[512,1024]{1,0:T(8,128)(2,1)}, bf16[512,1024]{1,0:T(8,128)(2,1)S(1)}, u32[]{:S(2)}, u32[]{:S(2)}) collective-permute-start(bf16[512,1024]{1,0:T(8,128)(2,1)} %bitcast.71), channel_id=1, source_target_pairs={{0,12},{4,0},{8,4},{12,8},{1,13},{5,1},{9,5},{13,9},{2,14},{6,2},{... | collective-permute-start | bytes 3145736 | tf_op jit(solution)/shard_map/ppermute | solution.py:163
  3.8 26.4 %collective-permute-start.9 = (bf16[512,1024]{1,0:T(8,128)(2,1)}, bf16[512,1024]{1,0:T(8,128)(2,1)S(1)}, u32[]{:S(2)}, u32[]{:S(2)}) collective-permute-start(bf16[512,1024]{1,0:T(8,128)(2,1)} %bitcast.72), channel_id=1, source_target_pairs={{0,4},{4,8},{8,12},{12,0},{1,5},{5,9},{9,13},{13,1},{2,6},{6,10},{... | collective-permute-start | bytes 3145736 | tf_op jit(solution)/shard_map/ppermute | solution.py:163
  5.2 27.2 %collective-permute-start.1 = (bf16[512,512]{1,0:T(8,128)(2,1)S(1)}, bf16[512,512]{1,0:T(8,128)(2,1)S(1)}, u32[]{:S(2)}, u32[]{:S(2)}) collective-permute-start(bf16[512,512]{1,0:T(8,128)(2,1)S(1)} %get-tuple-element.46), channel_id=1, source_target_pairs={{0,16},{16,32},{32,48},{48,0},{1,17},{17,33},{33,49},{49,1},{2,18}... | collective-permute-start | bytes 1572872 | tf_op jit(solution)/shard_map/ppermute | solution.py:163
  6.8 27.9 %collective-permute-start.2 = (bf16[512,512]{1,0:T(8,128)(2,1)S(1)}, bf16[512,512]{1,0:T(8,128)(2,1)S(1)}, u32[]{:S(2)}, u32[]{:S(2)}) collective-permute-start(bf16[512,512]{1,0:T(8,128)(2,1)S(1)} %get-tuple-element.46), channel_id=1, source_target_pairs={{0,48},{16,0},{32,16},{48,32},{1,49},{17,1},{33,17},{49,33},{2,50}... | collective-permute-start | bytes 1572872 | tf_op jit(solution)/shard_map/ppermute | solution.py:163
  26.6 14.0 %collective-permute-start.12 = (bf16[256,1024]{1,0:T(8,128)(2,1)S(1)}, bf16[256,1024]{1,0:T(8,128)(2,1)S(1)}, u32[]{:S(2)}, u32[]{:S(2)}) collective-permute-start(bf16[256,1024]{1,0:T(8,128)(2,1)S(1)} %slice.53), channel_id=1, source_target_pairs={{0,12},{4,0},{8,4},{12,8},{1,13},{5,1},{9,5},{13,9},{2,14},{6,2},{... | collective-permute-start | bytes 1572872 | tf_op jit(solution)/shard_map/ppermute | solution.py:163
  30.3 13.8 %collective-permute-start.11 = (bf16[256,1024]{1,0:T(8,128)(2,1)S(1)}, bf16[256,1024]{1,0:T(8,128)(2,1)S(1)}, u32[]{:S(2)}, u32[]{:S(2)}) collective-permute-start(bf16[256,1024]{1,0:T(8,128)(2,1)S(1)} %slice.52), channel_id=1, source_target_pairs={{0,4},{4,8},{8,12},{12,0},{1,5},{5,9},{9,13},{13,1},{2,6},{6,10},{... | collective-permute-start | bytes 1572872 | tf_op jit(solution)/shard_map/ppermute | solution.py:163
  30.4 16.1 %collective-permute-start.15 = (bf16[512,512]{1,0:T(8,128)(2,1)S(1)}, bf16[512,512]{1,0:T(8,128)(2,1)S(1)}, u32[]{:S(2)}, u32[]{:S(2)}) collective-permute-start(bf16[512,512]{1,0:T(8,128)(2,1)S(1)} %get-tuple-element.45), channel_id=1, source_target_pairs={{0,1},{1,64},{64,65},{65,0},{2,3},{3,66},{66,67},{67,2},{4,5},{5,6... | collective-permute-start | bytes 1572872 | tf_op jit(solution)/shard_map/ppermute | solution.py:163
  32.4 16.1 %collective-permute-start.16 = (bf16[512,512]{1,0:T(8,128)(2,1)S(1)}, bf16[512,512]{1,0:T(8,128)(2,1)S(1)}, u32[]{:S(2)}, u32[]{:S(2)}) collective-permute-start(bf16[512,512]{1,0:T(8,128)(2,1)S(1)} %get-tuple-element.45), channel_id=1, source_target_pairs={{0,65},{1,0},{64,1},{65,64},{2,67},{3,2},{66,3},{67,66},{4,69},{5,... | collective-permute-start | bytes 1572872 | tf_op jit(solution)/shard_map/ppermute | solution.py:163
  34.6 16.1 %collective-permute-start.3 = (bf16[256,512]{1,0:T(8,128)(2,1)S(1)}, bf16[256,512]{1,0:T(8,128)(2,1)S(1)}, u32[]{:S(2)}, u32[]{:S(2)}) collective-permute-start(bf16[256,512]{1,0:T(8,128)(2,1)S(1)} %slice.48), channel_id=1, source_target_pairs={{0,16},{16,32},{32,48},{48,0},{1,17},{17,33},{33,49},{49,1},{2,18}... | collective-permute-start | bytes 786440 | tf_op jit(solution)/shard_map/ppermute | solution.py:163
  46.5 151.6 %collective-permute-start.13 = (bf16[4,512,1024]{2,1,0:T(8,128)(2,1)}, bf16[4,512,1024]{2,1,0:T(8,128)(2,1)}, u32[]{:S(2)}, u32[]{:S(2)}) collective-permute-start(bf16[4,512,1024]{2,1,0:T(8,128)(2,1)} %pad_maximum_fusion.cot_own), channel_id=1, source_target_pairs={{0,2},{2,0},{1,3},{3,1},{4,6},{6,4},{5,7},{7,5},{8,10},{10,8},{9,1... | collective-permute-start | bytes 12582920 | tf_op jit(solution)/shard_map/ppermute | solution.py:287
  51.1 51.1 %collective-permute-start.6 = (bf16[4,512,512]{2,1,0:T(8,128)(2,1)S(1)}, bf16[4,512,512]{2,1,0:T(8,128)(2,1)S(1)}, u32[]{:S(2)}, u32[]{:S(2)}) collective-permute-start(bf16[4,512,512]{2,1,0:T(8,128)(2,1)S(1)} %pad_maximum_fusion.1.w0), channel_id=1, source_target_pairs={{0,65},{1,0},{64,1},{65,64},{2,67},{3,2},{66,3},{67,66},{4,69},{5,... | collective-permute-start | bytes 6291464 | tf_op jit(solution)/shard_map/ppermute | solution.py:163
  53.1 52.8 %collective-permute-start.5 = (bf16[4,512,512]{2,1,0:T(8,128)(2,1)S(1)}, bf16[4,512,512]{2,1,0:T(8,128)(2,1)S(1)}, u32[]{:S(2)}, u32[]{:S(2)}) collective-permute-start(bf16[4,512,512]{2,1,0:T(8,128)(2,1)S(1)} %pad_maximum_fusion.1.w0), channel_id=1, source_target_pairs={{0,1},{1,64},{64,65},{65,0},{2,3},{3,66},{66,67},{67,2},{4,5},{5,6... | collective-permute-start | bytes 6291464 | tf_op jit(solution)/shard_map/ppermute | solution.py:163
  58.1 52.3 %collective-permute-start.20 = (bf16[4,512,512]{2,1,0:T(8,128)(2,1)S(1)}, bf16[4,512,512]{2,1,0:T(8,128)(2,1)S(1)}, u32[]{:S(2)}, u32[]{:S(2)}) collective-permute-start(bf16[4,512,512]{2,1,0:T(8,128)(2,1)S(1)} %pad_maximum_fusion.2.w0), channel_id=1, source_target_pairs={{0,48},{16,0},{32,16},{48,32},{1,49},{17,1},{33,17},{49,33},{2,50}... | collective-permute-start | bytes 6291464 | tf_op jit(solution)/shard_map/ppermute | solution.py:163
  61.0 49.6 %collective-permute-start.19 = (bf16[4,512,512]{2,1,0:T(8,128)(2,1)S(1)}, bf16[4,512,512]{2,1,0:T(8,128)(2,1)S(1)}, u32[]{:S(2)}, u32[]{:S(2)}) collective-permute-start(bf16[4,512,512]{2,1,0:T(8,128)(2,1)S(1)} %pad_maximum_fusion.2.w0), channel_id=1, source_target_pairs={{0,16},{16,32},{32,48},{48,0},{1,17},{17,33},{33,49},{49,1},{2,18}... | collective-permute-start | bytes 6291464 | tf_op jit(solution)/shard_map/ppermute | solution.py:163
  102.2 27.2 %collective-permute-start = (bf16[512,1024]{1,0:T(8,128)(2,1)S(1)}, bf16[512,1024]{1,0:T(8,128)(2,1)S(1)}, u32[]{:S(2)}, u32[]{:S(2)}) collective-permute-start(bf16[512,1024]{1,0:T(8,128)(2,1)S(1)} %bitcast.61), channel_id=1, source_target_pairs={{0,16},{16,32},{32,48},{48,64},{64,80},{80,96},{96,112},{1,17},{17... | collective-permute-start | bytes 3145736 | tf_op jit(solution)/shard_map/ppermute | solution.py:169
  106.0 70.4 %collective-permute-start.8 = (bf16[2,512,512]{2,1,0:T(8,128)(2,1)S(1)}, bf16[2,512,512]{2,1,0:T(8,128)(2,1)}, u32[]{:S(2)}, u32[]{:S(2)}) collective-permute-start(bf16[2,512,512]{2,1,0:T(8,128)(2,1)S(1)} %slice.51), channel_id=1, source_target_pairs={{0,65},{1,0},{64,1},{65,64},{2,67},{3,2},{66,3},{67,66},{4,69},{5,... | collective-permute-start | bytes 3145736 | tf_op jit(solution)/shard_map/ppermute | solution.py:163
  110.5 87.6 %collective-permute-start.7 = (bf16[2,512,512]{2,1,0:T(8,128)(2,1)}, bf16[2,512,512]{2,1,0:T(8,128)(2,1)}, u32[]{:S(2)}, u32[]{:S(2)}) collective-permute-start(bf16[2,512,512]{2,1,0:T(8,128)(2,1)} %slice.50), channel_id=1, source_target_pairs={{0,1},{1,64},{64,65},{65,0},{2,3},{3,66},{66,67},{67,2},{4,5},{5,6... | collective-permute-start | bytes 3145736 | tf_op jit(solution)/shard_map/ppermute | solution.py:163
  110.6 98.7 %collective-permute-start.14 = (bf16[512,1024]{1,0:T(8,128)(2,1)S(1)}, bf16[512,1024]{1,0:T(8,128)(2,1)}, u32[]{:S(2)}, u32[]{:S(2)}) collective-permute-start(bf16[512,1024]{1,0:T(8,128)(2,1)S(1)} %bitcast.64), channel_id=1, source_target_pairs={{0,16},{16,32},{32,48},{48,64},{64,80},{80,96},{96,112},{1,17},{17... | collective-permute-start | bytes 3145736 | tf_op jit(solution)/shard_map/ppermute | solution.py:169
  129.4 93.2 %collective-permute-start.22 = (bf16[2,512,512]{2,1,0:T(8,128)(2,1)}, bf16[2,512,512]{2,1,0:T(8,128)(2,1)S(1)}, u32[]{:S(2)}, u32[]{:S(2)}) collective-permute-start(bf16[2,512,512]{2,1,0:T(8,128)(2,1)} %slice.57), channel_id=1, source_target_pairs={{0,48},{16,0},{32,16},{48,32},{1,49},{17,1},{33,17},{49,33},{2,50}... | collective-permute-start | bytes 3145736 | tf_op jit(solution)/shard_map/ppermute | solution.py:163
  176.3 46.2 %collective-permute-start.21 = (bf16[2,512,512]{2,1,0:T(8,128)(2,1)}, bf16[2,512,512]{2,1,0:T(8,128)(2,1)}, u32[]{:S(2)}, u32[]{:S(2)}) collective-permute-start(bf16[2,512,512]{2,1,0:T(8,128)(2,1)} %slice.56), channel_id=1, source_target_pairs={{0,16},{16,32},{32,48},{48,0},{1,17},{17,33},{33,49},{49,1},{2,18}... | collective-permute-start | bytes 3145736 | tf_op jit(solution)/shard_map/ppermute | solution.py:163
  253.8 22.0 %collective-permute-start.39 = (bf16[256,512]{1,0:T(8,128)(2,1)S(1)}, bf16[256,512]{1,0:T(8,128)(2,1)S(1)}, u32[]{:S(2)}, u32[]{:S(2)}) collective-permute-start(bf16[256,512]{1,0:T(8,128)(2,1)S(1)} %get-tuple-element.40), channel_id=1, source_target_pairs={{0,64},{1,65},{64,0},{65,1},{2,66},{3,67},{66,2},{67,3},{4,68},{5,... | collective-permute-start | bytes 786440 | tf_op jit(solution)/shard_map/ppermute | solution.py:163
  253.9 26.9 %collective-permute-start.41 = (bf16[256,512]{1,0:T(8,128)(2,1)S(1)}, bf16[256,512]{1,0:T(8,128)(2,1)S(1)}, u32[]{:S(2)}, u32[]{:S(2)}) collective-permute-start(bf16[256,512]{1,0:T(8,128)(2,1)S(1)} %get-tuple-element.41), channel_id=1, source_target_pairs={{0,65},{1,0},{64,1},{65,64},{2,67},{3,2},{66,3},{67,66},{4,69},{5,... | collective-permute-start | bytes 786440 | tf_op jit(solution)/shard_map/ppermute | solution.py:163
  257.8 23.6 %collective-permute-start.40 = (bf16[256,512]{1,0:T(8,128)(2,1)S(1)}, bf16[256,512]{1,0:T(8,128)(2,1)S(1)}, u32[]{:S(2)}, u32[]{:S(2)}) collective-permute-start(bf16[256,512]{1,0:T(8,128)(2,1)S(1)} %get-tuple-element.42), channel_id=1, source_target_pairs={{0,1},{1,64},{64,65},{65,0},{2,3},{3,66},{66,67},{67,2},{4,5},{5,6... | collective-permute-start | bytes 786440 | tf_op jit(solution)/shard_map/ppermute | solution.py:163
  269.7 100.4 %collective-permute-start.24 = (bf16[512,512]{1,0:T(8,128)(2,1)S(1)}, bf16[512,512]{1,0:T(8,128)(2,1)S(1)}, u32[]{:S(2)}, u32[]{:S(2)}) collective-permute-start(bf16[512,512]{1,0:T(8,128)(2,1)S(1)} %copy-done.21), channel_id=1, source_target_pairs={{16,0},{32,16},{48,32},{64,48},{80,64},{96,80},{112,96},{17,1},{33... | collective-permute-start | bytes 1572872 | tf_op jit(solution)/shard_map/ppermute | solution.py:169
  273.9 97.2 %collective-permute-start.26 = (bf16[512,512]{1,0:T(8,128)(2,1)S(1)}, bf16[512,512]{1,0:T(8,128)(2,1)S(1)}, u32[]{:S(2)}, u32[]{:S(2)}) collective-permute-start(bf16[512,512]{1,0:T(8,128)(2,1)S(1)} %copy-done.20), channel_id=1, source_target_pairs={{16,0},{32,16},{48,32},{64,48},{80,64},{96,80},{112,96},{17,1},{33... | collective-permute-start | bytes 1572872 | tf_op jit(solution)/shard_map/ppermute | solution.py:169
  280.8 26.9 %collective-permute-start.29 = (bf16[256,512]{1,0:T(8,128)(2,1)S(1)}, bf16[256,512]{1,0:T(8,128)(2,1)S(1)}, u32[]{:S(2)}, u32[]{:S(2)}) collective-permute-start(bf16[256,512]{1,0:T(8,128)(2,1)S(1)} %get-tuple-element.38), channel_id=1, source_target_pairs={{0,48},{16,0},{32,16},{48,32},{1,49},{17,1},{33,17},{49,33},{2,50}... | collective-permute-start | bytes 786440 | tf_op jit(solution)/shard_map/ppermute | solution.py:163
  281.4 26.3 %collective-permute-start.28 = (bf16[256,512]{1,0:T(8,128)(2,1)S(1)}, bf16[256,512]{1,0:T(8,128)(2,1)S(1)}, u32[]{:S(2)}, u32[]{:S(2)}) collective-permute-start(bf16[256,512]{1,0:T(8,128)(2,1)S(1)} %get-tuple-element.39), channel_id=1, source_target_pairs={{0,16},{16,32},{32,48},{48,0},{1,17},{17,33},{33,49},{49,1},{2,18}... | collective-permute-start | bytes 786440 | tf_op jit(solution)/shard_map/ppermute | solution.py:163
  288.0 22.0 %collective-permute-start.42 = (bf16[64,512]{1,0:T(8,128)(2,1)S(1)}, bf16[64,512]{1,0:T(8,128)(2,1)S(1)}, u32[]{:S(2)}, u32[]{:S(2)}) collective-permute-start(bf16[64,512]{1,0:T(8,128)(2,1)S(1)} %get-tuple-element.50), channel_id=1, source_target_pairs={{0,32},{16,48},{32,0},{48,16},{1,33},{17,49},{33,1},{49,17},{2,34}... | collective-permute-start | bytes 196616 | tf_op jit(solution)/shard_map/ppermute | solution.py:163
  318.5 54.3 %collective-permute-start.23 = (bf16[512,512]{1,0:T(8,128)(2,1)S(1)}, bf16[512,512]{1,0:T(8,128)(2,1)S(1)}, u32[]{:S(2)}, u32[]{:S(2)}) collective-permute-start(bf16[512,512]{1,0:T(8,128)(2,1)S(1)} %copy-done.19), channel_id=1, source_target_pairs={{16,0},{32,16},{48,32},{64,48},{80,64},{96,80},{112,96},{17,1},{33... | collective-permute-start | bytes 1572872 | tf_op jit(solution)/shard_map/ppermute | solution.py:169
  320.5 53.9 %collective-permute-start.25 = (bf16[512,512]{1,0:T(8,128)(2,1)S(1)}, bf16[512,512]{1,0:T(8,128)(2,1)S(1)}, u32[]{:S(2)}, u32[]{:S(2)}) collective-permute-start(bf16[512,512]{1,0:T(8,128)(2,1)S(1)} %copy-done.18), channel_id=1, source_target_pairs={{16,0},{32,16},{48,32},{64,48},{80,64},{96,80},{112,96},{17,1},{33... | collective-permute-start | bytes 1572872 | tf_op jit(solution)/shard_map/ppermute | solution.py:169
  329.7 15.4 %collective-permute-start.46 = (bf16[64,512]{1,0:T(8,128)(2,1)S(1)}, bf16[64,512]{1,0:T(8,128)(2,1)S(1)}, u32[]{:S(2)}, u32[]{:S(2)}) collective-permute-start(bf16[64,512]{1,0:T(8,128)(2,1)S(1)} %get-tuple-element.36), channel_id=1, source_target_pairs={{0,48},{16,0},{32,16},{48,32},{1,49},{17,1},{33,17},{49,33},{2,50}... | collective-permute-start | bytes 196616 | tf_op jit(solution)/shard_map/ppermute | solution.py:163
  372.7 14.3 %collective-permute-start.38 = (bf16[256,512]{1,0:T(8,128)(2,1)S(1)}, bf16[256,512]{1,0:T(8,128)(2,1)S(1)}, u32[]{:S(2)}, u32[]{:S(2)}) collective-permute-start(bf16[256,512]{1,0:T(8,128)(2,1)S(1)} %constant_dynamic-update-slice_fusion.12), channel_id=1, source_target_pairs={{0,32},{16,48},{32,0},{48,16},{1,33},{17,49},{33,1},{49,17},{2,34}... | collective-permute-start | bytes 786440 | tf_op jit(solution)/shard_map/ppermute | solution.py:163
  (47 other events, 739.2 us)
